TPU v7x, 32 devices: a whole 2x2x4 slice. The times are simulated.
32 devices in a mesh: dp: 2 (over core), seq: 4 (over z), head: 4 (over y, x).
Axes of the slice: x: 2, y: 2, z: 4, core: 2. Of those that a mesh axis runs over, the one named last changes fastest.
Arguments:
- x_in: float32 [2, 512, 1024], P('dp', 'seq'), may hold values from -6 to 6
- cotangent: float32 [2, 512, 1024], P('dp', 'seq'), may hold values from -6 to 6
- attn_gain: bfloat16 [1024], P('seq'), may hold values from 0.25 to 1.75
- w_query: bfloat16 [1024, 512], P('seq', 'head'), may hold values from -0.1875 to 0.1875
- w_key: bfloat16 [1024, 512], P('seq', 'head'), may hold values from -0.1875 to 0.1875
- w_value: bfloat16 [1024, 1024], P('seq', 'head'), may hold values from -0.1875 to 0.1875
- w_outgate: bfloat16 [1024, 1024], P('seq', 'head'), may hold values from -0.1875 to 0.1875
- w_lowrank: bfloat16 [1024, 16], P('seq'), may hold values from -0.1875 to 0.1875
- w_forget: float32 [16, 512], replicated, may hold values from -1.5 to 1.5
- forget_bias: float32 [512], replicated, may hold values from -1 to 6
- group_gain: float32 [256], replicated, may hold values from 0.25 to 1.75
- w_output: bfloat16 [1024, 1024], P('head', 'seq'), may hold values from -0.375 to 0.375
- mlp_gain: bfloat16 [1024], P('seq'), may hold values from 0.25 to 1.75
- w_gate: bfloat16 [1024, 2816], P('seq', 'head'), may hold values from -0.1875 to 0.1875
- w_up: bfloat16 [1024, 2816], P('seq', 'head'), may hold values from -0.1875 to 0.1875
- w_down: bfloat16 [2816, 1024], P('head', 'seq'), may hold values from -0.109375 to 0.109375
Outputs:
- block_out: float32 [2, 512, 1024], P('dp', 'seq')
- grad_input: float32 [2, 512, 1024], P('dp', 'seq')
- grad_attn_gain: float32 [1024], P('seq')
- grad_query: float32 [1024, 512], P('seq', 'head')
- grad_key: float32 [1024, 512], P('seq', 'head')
- grad_value: float32 [1024, 1024], P('seq', 'head')
- grad_outgate: float32 [1024, 1024], P('seq', 'head')
- grad_lowrank: float32 [1024, 16], P('seq')
- grad_forget: float32 [16, 512], replicated
- grad_bias: float32 [512], replicated
- grad_group_gain: float32 [256], replicated
- grad_output: float32 [1024, 1024], P('head', 'seq')
- grad_mlp_gain: float32 [1024], P('seq')
- grad_gate: float32 [1024, 2816], P('seq', 'head')
- grad_up: float32 [1024, 2816], P('seq', 'head')
- grad_down: float32 [2816, 1024], P('head', 'seq')
All inputs are finite; a program needn't handle non-finite values.
Results may differ from a plain program's by a relative error of at most 0.0097.
Values may be sent and summed in bfloat16 or wider, within the bound.
A program may use at most 128 MiB of HBM per device.

v0:
```python
import jax
import jax.numpy as jnp
from jax import lax
from jax.experimental import pallas as pl
from jax.experimental.pallas import tpu as pltpu
from jax.sharding import PartitionSpec as P

DK = 128
DV = 256
SPAN = 64


epsilon = 1e-06
normalizer = 16.0
highest = lax.Precision.HIGHEST


def exchange(items, cid):
    groups = []
    for kind, axis, _ in items:
        for name in axis if kind in ("wg", "rs") else (axis,):
            if name not in groups:
                groups.append(name)
    names = []
    for group in groups:
        for name in group if isinstance(group, tuple) else (group,):
            if name not in names:
                names.append(name)
    size = {name: lax.axis_size(name) for name in names}
    for group in groups:
        if isinstance(group, tuple):
            size[group] = size[group[0]] * size[group[1]]
    out_shape, scratch = [], []
    dma = pltpu.SemaphoreType.DMA
    for kind, axis, arr in items:
        if kind in ("wg", "rs"):
            n, m = size[axis[0]], size[axis[1]]
            scratch += [dma((2, 2, n)), dma((2, 2, n, m))]
            if kind == "wg":
                out_shape.append(jax.ShapeDtypeStruct((n,) + arr.shape, arr.dtype))
                scratch.append(dma)
            else:
                out_shape.append(jax.ShapeDtypeStruct((m,) + arr.shape[1:], jnp.float32))
                scratch.append(pltpu.VMEM((2,) + arr.shape, arr.dtype))
                scratch.append(pltpu.VMEM((2,) + arr.shape, arr.dtype))
            continue
        n = size[axis]
        scratch.append(dma((2, n)))
        if kind == "ar":
            out_shape.append(jax.ShapeDtypeStruct(arr.shape, arr.dtype))
            scratch += [dma((2, n)), pltpu.VMEM(arr.shape, arr.dtype)]
        else:
            inner = arr.shape if kind == "ag" else arr.shape[1:]
            out_shape.append(jax.ShapeDtypeStruct((n,) + inner, arr.dtype))
            scratch.append(dma)

    def kernel(*refs):
        count = len(items)
        ins, outs, rest = refs[:count], refs[count : 2 * count], list(refs[2 * count :])
        me = {name: lax.axis_index(name) for name in names}
        for group in groups:
            if isinstance(group, tuple):
                me[group] = me[group[0]] * size[group[1]] + me[group[1]]

        def device(group, place):
            if isinstance(group, tuple):
                return {
                    group[0]: place // size[group[1]],
                    group[1]: lax.rem(place, size[group[1]]),
                }
            return {group: place}

        barrier = pltpu.get_barrier_semaphore()
        for group in groups:
            for k in range(1, size[group]):
                pl.semaphore_signal(
                    barrier,
                    inc=1,
                    device_id=device(group, lax.rem(me[group] + k, size[group])),
                    device_id_type=pl.DeviceIdType.MESH,
                )
        pl.semaphore_wait(barrier, sum(size[group] - 1 for group in groups))

        def remote(source, target, send, recv, group, place):
            return pltpu.make_async_remote_copy(
                src_ref=source,
                dst_ref=target,
                send_sem=send,
                recv_sem=recv,
                device_id=device(group, place),
                device_id_type=pl.DeviceIdType.MESH,
            )

        waits, chains, sums = [], [], []

        def chain_gather(src, dst, sems, sems_two, local, axis, arr):
            name, other = axis
            n, here, m, place = size[name], me[name], size[other], me[other]
            part = arr.shape[0] // m
            rows = pl.ds(pl.multiple_of(place * part, part), part)
            own = pltpu.make_async_copy(src, dst.at[here], local)
            own.start()
            waits.append(own.wait)

            def hop(way, step, source, index):
                to = here + 1 if way == 0 else here - 1
                return remote(
                    source,
                    dst.at[index, rows],
                    sems.at[way, 0, step],
                    sems.at[way, 1, step],
                    name,
                    to,
                )

            def guarded(ok, call):
                waits.append(lambda: pl.when(ok)(call))

            open_ends = (here < n - 1, here > 0)
            for way in range(2):
                @pl.when(open_ends[way])
                def _():
                    hop(way, 0, src.at[rows], here).start()

                guarded(
                    open_ends[way],
                    lambda way=way: hop(way, 0, src.at[rows], here).wait_send(),
                )

            def advance(step):
                for way in range(2):
                    came = here - 1 - step if way == 0 else here + 1 + step
                    ok = came >= 0 if way == 0 else came < n
                    on = jnp.logical_and(ok, open_ends[way])

                    def partners(way=way, came=came):
                        for j in range(1, m):
                            to = lax.rem(place + j, m)
                            whose = lax.rem(place + m - j, m)
                            piece = dst.at[came, rows]
                            theirs = dst.at[came, pl.ds(pl.multiple_of(whose * part, part), part)]
                            send, recv = sems_two.at[way, 0, step, j], sems_two.at[way, 1, step, j]
                            yield (
                                remote(piece, piece, send, recv, other, to),
                                remote(theirs, theirs, send, recv, other, to),
                            )

                    @pl.when(ok)
                    def _():
                        hop(way, step, dst.at[came, rows], came).wait_recv()

                    if step + 1 < n - 1:
                        @pl.when(on)
                        def _():
                            hop(way, step + 1, dst.at[came, rows], came).start()

                        guarded(
                            on,
                            lambda way=way, came=came: hop(
                                way, step + 1, dst.at[came, rows], came
                            ).wait_send(),
                        )

                    @pl.when(ok)
                    def _():
                        for copy, _ in partners():
                            copy.start()

                    def finish(partners=partners):
                        for copy, arrival in partners():
                            copy.wait_send()
                            arrival.wait_recv()

                    guarded(ok, finish)

            chains.append((n - 1, advance, lambda: None))

        def chain_sum(src, dst, sems, sems_two, land, held, axis, arr):
            name, other = axis
            n, here, m, place = size[name], me[name], size[other], me[other]
            tall = 16 if arr.shape[1] % 16 == 0 else arr.shape[1]
            turns = arr.shape[1] // tall

            def by_rows(call):
                def one(turn, carry):
                    call(pl.ds(pl.multiple_of(turn * tall, tall), tall))
                    return carry

                lax.fori_loop(0, turns, one, 0)

            def hop(way, step, source, index):
                to = here + 1 if way == 0 else here - 1
                return remote(
                    source,
                    land.at[way, index],
                    sems.at[way, 0, step],
                    sems.at[way, 1, step],
                    name,
                    to,
                )

            def guarded(ok, call):
                waits.append(lambda: pl.when(ok)(call))

            firsts = (here == 0, here == n - 1)

            def advance(step):
                for way in range(2):
                    goal = n - 1 - step if way == 0 else step
                    passing = here < goal if way == 0 else here > goal
                    inner = jnp.logical_and(passing, jnp.logical_not(firsts[way]))
                    first = jnp.logical_and(passing, firsts[way])

                    @pl.when(first)
                    def _():
                        if step > 0:
                            before = goal + 1 if way == 0 else goal - 1
                            hop(way, step - 1, src.at[before], before).wait_send()
                        hop(way, step, src.at[goal], goal).start()

                    if step == n - 2:
                        guarded(
                            first,
                            lambda way=way, goal=goal: hop(
                                way, step, src.at[goal], goal
                            ).wait_send(),
                        )

                    @pl.when(inner)
                    def _():
                        hop(way, step, land.at[way, goal], goal).wait_recv()

                        def add(rows):
                            held[way, goal, rows] = (
                                land[way, goal, rows].astype(jnp.float32)
                                + src[goal, rows].astype(jnp.float32)
                            ).astype(held.dtype)

                        by_rows(add)
                        hop(way, step, held.at[way, goal], goal).start()

                    guarded(
                        inner,
                        lambda way=way, goal=goal: hop(
                            way, step, held.at[way, goal], goal
                        ).wait_send(),
                    )

            def partners():
                for j in range(1, m):
                    to = lax.rem(place + j, m)
                    whose = lax.rem(place + m - j, m)
                    send, recv = sems_two.at[0, 0, 0, j], sems_two.at[0, 1, 0, j]
                    yield (
                        remote(dst.at[place], dst.at[place], send, recv, other, to),
                        remote(dst.at[whose], dst.at[whose], send, recv, other, to),
                    )

            def close():
                def start(rows):
                    dst[place, rows] = src[here, rows].astype(jnp.float32)

                by_rows(start)
                for way in range(2):
                    step = n - 1 - here if way == 0 else here

                    @pl.when(jnp.logical_not(firsts[way]))
                    def _():
                        hop(way, step, land.at[way, here], here).wait_recv()

                        def add(rows):
                            dst[place, rows] = dst[place, rows] + land[way, here, rows].astype(
                                jnp.float32
                            )

                        by_rows(add)

                for copy, _ in partners():
                    copy.start()
                for copy, arrival in partners():
                    waits.append(copy.wait_send)
                    waits.append(arrival.wait_recv)

            chains.append((n, advance, close))

        for (kind, axis, arr), src, dst in zip(items, ins, outs):
            if kind in ("wg", "rs"):
                extra = [rest.pop(0) for _ in range(3 if kind == "wg" else 4)]
                (chain_gather if kind == "wg" else chain_sum)(src, dst, *extra, axis, arr)
                continue
            sems = rest.pop(0)
            n, here = size[axis], me[axis]
            if kind == "ar":
                sems_two, land = rest.pop(0), rest.pop(0)
                sent = []
                for k in range(1, n):
                    peer = lax.rem(here + k, n)
                    came = lax.rem(here + n - k, n)
                    pair = sems.at[0, k], sems.at[1, k]
                    copy = remote(src.at[peer], land.at[here], *pair, axis, peer)
                    copy.start()
                    sent.append((copy, remote(land.at[came], land.at[came], *pair, axis, peer)))
                sums.append((src, dst, land, sems_two, axis, n, here, sent))
                continue
            local = rest.pop(0)

            def piece(place):
                if kind == "ag":
                    return src
                if isinstance(axis, tuple):
                    return src.at[place // size[axis[1]]]
                return src.at[place]

            own = pltpu.make_async_copy(piece(here), dst.at[here], local)
            own.start()
            waits.append(own.wait)
            for k in range(1, n):
                peer = lax.rem(here + k, n)
                came = lax.rem(here + n - k, n)
                pair = sems.at[0, k], sems.at[1, k]
                copy = remote(piece(peer), dst.at[here], *pair, axis, peer)
                copy.start()
                waits.append(copy.wait_send)
                waits.append(remote(dst.at[came], dst.at[came], *pair, axis, peer).wait_recv)

        def finish_sums():
            for src, dst, land, sems_two, axis, n, here, sent in sums:
                total = src[here].astype(jnp.float32)
                for k, (copy, arrival) in enumerate(sent, 1):
                    arrival.wait_recv()
                    total = total + land[lax.rem(here + n - k, n)].astype(jnp.float32)
                dst[here] = total.astype(dst.dtype)
                for k in range(1, n):
                    peer = lax.rem(here + k, n)
                    came = lax.rem(here + n - k, n)
                    pair = sems_two.at[0, k], sems_two.at[1, k]
                    copy = remote(dst.at[here], dst.at[here], *pair, axis, peer)
                    copy.start()
                    waits.append(copy.wait_send)
                    waits.append(
                        remote(dst.at[came], dst.at[came], *pair, axis, peer).wait_recv
                    )
                for copy, _ in sent:
                    waits.append(copy.wait_send)

        steps = max([entry[0] for entry in chains], default=0)
        for step in range(steps):
            if step == 1:
                finish_sums()
            for last, advance, _ in chains:
                if step < last:
                    advance(step)
        if steps < 2:
            finish_sums()
        for _, _, close in chains:
            close()
        for wait in waits:
            wait()

    def room(shape, dtype):
        item = jnp.dtype(dtype).itemsize
        lead = 1
        for extent in shape[:-2]:
            lead *= extent
        tile = 32 // item
        return lead * (-(-shape[-2] // tile) * tile) * (-(-shape[-1] // 128) * 128) * item

    total = sum(room(item[2].shape, item[2].dtype) for item in items)
    total += sum(room(shape.shape, shape.dtype) for shape in out_shape)
    for kind, _, arr in items:
        total += room(arr.shape, arr.dtype) * {"ar": 3, "rs": 4}.get(kind, 0)
    limit = min(60 * 2**20, total + total // 8 + 2 * 2**20)
    vmem = pl.BlockSpec(memory_space=pltpu.VMEM)
    return pl.pallas_call(
        kernel,
        out_shape=out_shape,
        in_specs=[vmem] * len(items),
        out_specs=[vmem] * len(items),
        scratch_shapes=scratch,
        compiler_params=pltpu.CompilerParams(
            collective_id=cid, has_side_effects=True, vmem_limit_bytes=limit
        ),
    )(*[item[2] for item in items])


def dot_t(left, right):
    return lax.dot_general(
        left, right, (((1,), (1,)), ((), ())), preferred_element_type=jnp.float32
    )


def dot_rows(left, right):
    return lax.dot_general(
        left, right, (((0,), (0,)), ((), ())), preferred_element_type=jnp.float32
    )


def product(left, right):
    return jnp.dot(left, right, preferred_element_type=jnp.float32)


def rms_rows(inputs):
    return lax.rsqrt(jnp.mean(inputs * inputs, axis=-1, keepdims=True) + epsilon)


def norm_back(inputs, scale, gain, grad):
    scaled = gain * grad
    gain_terms = grad * inputs * scale
    input_grad = scale * scaled - inputs * scale**3 * jnp.mean(
        scaled * inputs, axis=-1, keepdims=True
    )
    return (gain_terms, input_grad)


def mixer_block(queries, keys_in, values_in, log_decay, start_state):
    block_len = min(SPAN, queries.shape[0])
    blocks = queries.shape[0] // block_len

    def cut(array):
        return array.reshape(blocks, block_len, array.shape[-1])

    lower = jnp.tril(jnp.ones((block_len, block_len), jnp.float32))

    def block_step(carried, pieces):
        query_blk, key_blk, value_blk, decay_blk = pieces
        running = jnp.cumsum(decay_blk, axis=0)
        from_state = jnp.dot(query_blk * jnp.exp(running), carried, precision=highest)
        spread = (
            jnp.exp(jnp.minimum(running[:, None, :] - running[None, :, :], 0.0)) * lower[:, :, None]
        )
        scores = jnp.einsum("id,jd,ijd->ij", query_blk, key_blk, spread, precision=highest)
        inside = jnp.dot(scores, value_blk, precision=highest)
        ending = running[-1]
        weighted = key_blk * jnp.exp(ending[None, :] - running)
        carried = jnp.exp(ending)[:, None] * carried + jnp.dot(
            weighted.T, value_blk, precision=highest
        )
        return (carried, from_state + inside)

    final_state, outputs = lax.scan(
        jax.checkpoint(block_step),
        start_state,
        (cut(queries), cut(keys_in), cut(values_in), cut(log_decay)),
    )
    return (outputs.reshape(queries.shape[0], values_in.shape[-1]), final_state)


def on_device(
    x_in,
    cotangent,
    attn_gain,
    w_query,
    w_key,
    w_value,
    w_outgate,
    w_lowrank,
    w_forget,
    forget_bias,
    group_gain,
    w_output,
    mlp_gain,
    w_gate,
    w_up,
    w_down,
):
    seqs_here, tok_here, width = x_in.shape
    total_rows = seqs_here * tok_here
    bf16, f32 = jnp.bfloat16, jnp.float32
    n_seq, n_head, n_dp = lax.axis_size("seq"), lax.axis_size("head"), lax.axis_size("dp")
    seq_pos, head_pos = lax.axis_index("seq"), lax.axis_index("head")
    shard_rows = w_query.shape[0]
    part_rows = shard_rows // n_dp
    key_cols, val_cols, hidden = w_query.shape[1], w_value.shape[1], w_gate.shape[1]
    rank = w_lowrank.shape[1]
    heads_here = key_cols // DK
    head_scale = DK ** (-0.5)
    side = -(-(rank + 2) // 128) * 128
    packed = jnp.concatenate(
        (
            w_query,
            w_key,
            w_value,
            w_outgate,
            w_lowrank,
            attn_gain[:, None],
            mlp_gain[:, None],
            jnp.zeros((shard_rows, side - rank - 2), bf16),
            w_output.T,
        ),
        axis=1,
    )
    packed_mlp = jnp.concatenate((w_gate, w_up, w_down.T), axis=1)
    (weights,) = exchange([("wg", ("seq", "dp"), packed)], 0)
    weights = weights.reshape(width, -1)
    attn_cols = 2 * key_cols + 2 * val_cols
    w_attn = weights[:, :attn_cols]
    w_low = weights[:, attn_cols : attn_cols + side]
    wl_full = w_low[:, :rank]
    gain_first = w_low[:, rank].astype(f32)
    gain_second = w_low[:, rank + 1].astype(f32)
    at = attn_cols + side
    wo_t = weights[:, at : at + val_cols]
    forget_cols = lax.dynamic_slice_in_dim(w_forget, head_pos * key_cols, key_cols, 1)
    bias_cols = lax.dynamic_slice_in_dim(forget_bias, head_pos * key_cols, key_cols, 0)

    def heads_of(array, size):
        return array.reshape(seqs_here, tok_here, heads_here, size).transpose(0, 2, 1, 3)

    def rows_of(array):
        return array.transpose(0, 2, 1, 3).reshape(total_rows, -1)

    def spread_head(array):
        return array.astype(bf16).reshape(n_head, array.shape[0] // n_head, array.shape[1])

    def by_part(array):
        array = array.reshape(total_rows, n_seq, n_dp, part_rows)
        return array.transpose(2, 0, 1, 3).reshape(n_dp, total_rows, n_seq * part_rows)

    def all_rows(array):
        return array.reshape(n_dp * total_rows, -1)

    def grad_of(left, right):
        return dot_rows(all_rows(left), all_rows(right)).astype(bf16)

    flat_in = x_in.reshape(total_rows, width)
    flat_cot = cotangent.reshape(total_rows, width)
    scale_one = rms_rows(flat_in)
    normed_in = (flat_in * scale_one * gain_first).astype(bf16)
    proj = product(normed_in, w_attn)
    q_rows = proj[:, :key_cols]
    k_rows = proj[:, key_cols : 2 * key_cols]
    v_rows = proj[:, 2 * key_cols : 2 * key_cols + val_cols]
    og_rows = proj[:, 2 * key_cols + val_cols :]
    low_rank = product(normed_in, wl_full)
    pre_gate = jnp.dot(low_rank, forget_cols, precision=highest) + bias_cols
    log_decay = jax.nn.log_sigmoid(pre_gate) / normalizer
    q_heads = heads_of(q_rows, DK)
    k_heads = heads_of(k_rows, DK)
    v_heads = heads_of(v_rows, DV)
    decay_heads = heads_of(log_decay, DK)
    running = jnp.cumsum(decay_heads, axis=2)
    ending = running[:, :, -1, :]
    decay_total = jnp.exp(ending)
    local_state = jnp.einsum(
        "shld,shlv->shdv",
        k_heads * jnp.exp(ending[:, :, None, :] - running),
        v_heads,
        precision=highest,
    )
    state_shape = local_state.shape
    states, decays = exchange(
        [
            ("ag", "seq", local_state.astype(bf16).reshape(-1, DV)),
            ("ag", "seq", jnp.broadcast_to(decay_total.reshape(1, -1), (8, decay_total.size))),
        ],
        1,
    )
    decays = decays[:, 0].reshape((n_seq,) + decay_total.shape)
    states = states.reshape((n_seq,) + state_shape)
    start_state = jnp.zeros(state_shape, f32)
    for j in range(n_seq - 1):
        start_state = jnp.where(
            j < seq_pos, decays[j][..., None] * start_state + states[j].astype(f32), start_state
        )

    def mixed(q_part, k_part, v_part, d_part):
        return jax.vmap(jax.vmap(mixer_block))(
            q_part * head_scale, k_part, v_part, d_part, start_state
        )

    (o_heads, end_state), pullback = jax.vjp(mixed, q_heads, k_heads, v_heads, decay_heads)
    gate_heads = heads_of(og_rows, DV)
    scale_three = rms_rows(o_heads)
    gated_norm = o_heads * scale_three * group_gain
    gate_sig = jax.nn.sigmoid(gate_heads)
    gate_act = gate_heads * gate_sig
    mixed_out = rows_of(gated_norm * gate_act).astype(bf16)
    mix_sum, weights_mlp = exchange(
        [
            ("ar", "head", spread_head(dot_t(mixed_out, wo_t))),
            ("wg", ("seq", "dp"), packed_mlp),
        ],
        2,
    )
    weights_mlp = weights_mlp.reshape(width, -1)
    w_gu = weights_mlp[:, : 2 * hidden]
    wdown_t = weights_mlp[:, 2 * hidden :]
    resid = flat_in + mix_sum.reshape(total_rows, width).astype(f32)
    scale_two = rms_rows(resid)
    normed_mid = (resid * scale_two * gain_second).astype(bf16)
    both = product(normed_mid, w_gu)
    gate_pre, up_pre = both[:, :hidden], both[:, hidden:]
    gate_sigma = jax.nn.sigmoid(gate_pre)
    gate_silu = gate_pre * gate_sigma
    mlp_hidden = (gate_silu * up_pre).astype(bf16)
    grad_out_b = flat_cot.astype(bf16)
    d_hidden = product(grad_out_b, wdown_t)
    d_gate_pre = (d_hidden * up_pre * gate_sigma * (1.0 + gate_pre * (1.0 - gate_sigma))).astype(
        bf16
    )
    d_up_pre = (d_hidden * gate_silu).astype(bf16)
    d_both = jnp.concatenate((d_gate_pre, d_up_pre), axis=1)
    sums, mid_two, out_two, both_two, hidden_two = exchange(
        [
            (
                "ar",
                "head",
                spread_head(
                    jnp.concatenate((dot_t(mlp_hidden, wdown_t), dot_t(d_both, w_gu)), axis=0)
                ),
            ),
            ("a2a", "dp", by_part(normed_mid)),
            ("a2a", "dp", by_part(grad_out_b)),
            ("ag", "dp", d_both),
            ("ag", "dp", mlp_hidden),
        ],
        3,
    )
    sums = sums.reshape(2, total_rows, width).astype(f32)
    result = resid + sums[0]
    d_normed_mid = sums[1]
    gain_terms, d_resid_norm = norm_back(resid, scale_two, gain_second, d_normed_mid)
    d_gain_two = jnp.sum(gain_terms, axis=0)
    d_resid = flat_cot + d_resid_norm
    d_resid_b = d_resid.astype(bf16)
    d_mixed = heads_of(product(d_resid_b, wo_t), DV)
    d_norm_out = d_mixed * gate_act
    d_gate_heads = d_mixed * gated_norm * gate_sig * (1.0 + gate_heads * (1.0 - gate_sig))
    d_group = jnp.sum(d_norm_out * o_heads * scale_three, axis=(0, 1, 2))
    group_terms, d_o_heads = norm_back(o_heads, scale_three, group_gain, d_norm_out)
    state_grad = jnp.einsum(
        "shld,shlv->shdv", q_heads * head_scale * jnp.exp(running), d_o_heads, precision=highest
    )
    grads_in, mixed_two, resid_two = exchange(
        [
            ("ag", "seq", state_grad.astype(bf16).reshape(-1, DV)),
            ("ag", "dp", mixed_out),
            ("a2a", "dp", by_part(d_resid_b)),
        ],
        4,
    )
    grads_late = jnp.concatenate(
        (
            grad_of(resid_two, mixed_two),
            grad_of(mid_two, both_two),
            grad_of(out_two, hidden_two),
        ),
        axis=1,
    ).reshape(n_seq, part_rows, -1)
    grads_in = grads_in.reshape((n_seq,) + state_shape)
    later_grad = jnp.zeros(state_shape, f32)
    for j in range(n_seq - 1, 0, -1):
        later_grad = jnp.where(
            j > seq_pos, decays[j][..., None] * later_grad + grads_in[j].astype(f32), later_grad
        )
    d_q, d_k, d_v, d_decay = pullback((d_o_heads, later_grad))
    d_pre = rows_of(d_decay) / normalizer * jax.nn.sigmoid(-pre_gate)
    d_bias = jnp.sum(d_pre, axis=0)
    d_forget = jnp.dot(low_rank.T, d_pre, precision=highest)
    d_low_part = jnp.dot(d_pre, forget_cols.T, precision=highest)
    d_proj = jnp.concatenate(
        (
            rows_of(d_q).astype(bf16),
            rows_of(d_k).astype(bf16),
            rows_of(d_v).astype(bf16),
            rows_of(d_gate_heads).astype(bf16),
        ),
        axis=1,
    )
    d_in_part = jnp.concatenate(
        (dot_t(d_proj, w_attn), d_low_part, jnp.zeros((total_rows, side - rank), f32)), axis=1
    )
    group_rows = d_group.reshape(1, DV)
    if DV < key_cols:
        group_rows = jnp.pad(group_rows, ((0, 0), (0, key_cols - DV)))
    if DV > key_cols:
        group_rows = group_rows.reshape(-1, key_cols)
    used = rank + 1 + group_rows.shape[0]
    small = jnp.concatenate(
        (
            d_forget,
            d_bias[None, :],
            group_rows,
            jnp.zeros((-used % 8, key_cols), f32),
        ),
        axis=0,
    )
    grads_late, in_sum, small_all, in_two, proj_two = exchange(
        [
            ("rs", ("seq", "dp"), grads_late),
            ("ar", "head", spread_head(d_in_part)),
            ("ag", ("seq", "dp"), small),
            ("a2a", "dp", by_part(normed_in)),
            ("ag", "dp", d_proj),
        ],
        5,
    )
    in_sum = in_sum.reshape(total_rows, width + side)
    d_low_b = in_sum[:, width : width + rank]
    d_normed_in = in_sum[:, :width].astype(f32) + dot_t(d_low_b, wl_full)
    first_terms, d_in_norm = norm_back(flat_in, scale_one, gain_first, d_normed_in)
    d_gain_one = jnp.sum(first_terms, axis=0)
    grad_in = d_resid + d_in_norm

    grads_attn = grad_of(in_two, proj_two).reshape(n_seq, part_rows, -1)
    tall = jnp.concatenate(
        (
            dot_rows(d_low_b, normed_in),
            d_gain_one[None, :],
            d_gain_two[None, :],
            jnp.zeros((-(rank + 2) % 8, width), f32),
        ),
        axis=0,
    )
    tall = tall.reshape(-1, n_seq, shard_rows).transpose(1, 0, 2)
    grads_attn, tall, small = exchange(
        [
            ("rs", ("seq", "dp"), grads_attn),
            ("a2a", ("seq", "dp"), tall),
            ("ag", "head", jnp.sum(small_all, axis=0)),
        ],
        6,
    )
    grads_attn = grads_attn.reshape(shard_rows, -1)
    grads_late = grads_late.reshape(shard_rows, -1)
    tall = jnp.sum(tall, axis=0)
    s_forget = small[:, :rank].transpose(1, 0, 2).reshape(rank, -1)
    s_bias = small[:, rank].reshape(-1)
    s_group = jnp.sum(small[:, rank + 1 : used], axis=0).reshape(-1)[:DV]
    s_query, s_key, s_value, s_outgate = jnp.split(
        grads_attn, [key_cols, 2 * key_cols, 2 * key_cols + val_cols], axis=1
    )
    s_output, s_gate, s_up, s_down = jnp.split(
        grads_late, [val_cols, val_cols + hidden, val_cols + 2 * hidden], axis=1
    )
    return (
        result.reshape(seqs_here, tok_here, width),
        grad_in.reshape(seqs_here, tok_here, width),
        tall[rank],
        s_query,
        s_key,
        s_value,
        s_outgate,
        tall[:rank].T,
        s_forget,
        s_bias,
        s_group,
        s_output.T,
        tall[rank + 1],
        s_gate,
        s_up,
        s_down.T,
    )


def solution(mesh):
    return jax.shard_map(
        on_device,
        mesh=mesh,
        in_specs=(
            P("dp", "seq", None),
            P("dp", "seq", None),
            P("seq"),
            P("seq", "head"),
            P("seq", "head"),
            P("seq", "head"),
            P("seq", "head"),
            P("seq", None),
            P(),
            P(),
            P(),
            P("head", "seq"),
            P("seq"),
            P("seq", "head"),
            P("seq", "head"),
            P("head", "seq"),
        ),
        out_specs=(
            P("dp", "seq", None),
            P("dp", "seq", None),
            P("seq"),
            P("seq", "head"),
            P("seq", "head"),
            P("seq", "head"),
            P("seq", "head"),
            P("seq", None),
            P(),
            P(),
            P(),
            P("head", "seq"),
            P("seq"),
            P("seq", "head"),
            P("seq", "head"),
            P("head", "seq"),
        ),
        check_vma=False,
    )
```

profile of v0, /device:TPU:0, one launch (start us, length us, event | category | flops | bytes accessed | tf_op | source)
XLA Modules:
  0.0 338.7 jit_solution(15920169999136778679)
XLA Ops:
  5.2 28.1 %shard_map.279 = bf16[4,256,1152]{2,1,0:T(8,128)(2,1)S(1)} custom-call(bf16[256,1152]{1,0:T(8,128)(2,1)S(1)} %concatenate.39.refs_0_), custom_call_target="tpu_custom_call" | custom-call | tf_op jit(solution)/shard_map/pallas_call | solution.py:374
  38.3 10.0 %shard_map.280 = (bf16[4,128,256]{2,1,0:T(8,128)(2,1)S(1)}, f32[4,8,128]{2,1,0:T(8,128)S(1)}) custom-call(bf16[128,256]{1,0:T(8,128)(2,1)S(1)} %convolution_convert_fusion.2.refs_0_, f32[8,128]{1,0:T(8,128)S(1)} %broadcast_in_dim.117.refs_1_), custom_call_target="tpu_custom_call" | custom-call | tf_op jit(solution)/shard_map/pallas_call | solution.py:374
  50.9 6.8 %while.40 = (s32[]{:T(128)}, f32[1,1,128,256]{3,2,1,0:T(8,128)S(1)}, f32[2,1,1,64,256]{4,3,2,1,0:T(8,128)S(1)}, f32[2,1,1,128,256]{4,3,2,1,0:T(8,128)S(1)}, f32[...) while((s32[]{:T(128)}, ...), condition=%wide.region_4.5_spmd.clone.clone, body=%wide.region_2.4_spmd.clone.sunk.clone | while | flops 66686976 | bytes 5756017 | solution.py:440
  66.3 2.6 concatenate.40.refs_1_
  69.8 42.0 %shard_map.281 = (bf16[4,32,1024]{2,1,0:T(8,128)(2,1)S(1)}, bf16[4,256,2112]{2,1,0:T(8,128)(2,1)S(1)}) custom-call(bf16[4,32,1024]{2,1,0:T(8,128)(2,1)S(1)} %bitcast.657, bf16[256,2112]{1,0:T(8,128)(2,1)S(1)} %concatenate.40.refs_1_), custom_call_target="tpu_custom_call" | custom-call | tf_op jit(solution)/shard_map/pallas_call | solution.py:374
  111.8 2.1 copy-done.20
  117.8 2.5 fusion.78
  120.3 2.0 multiply_convert_fusion.4
  124.8 2.1 copy.213
  130.2 2.0 copy_bitcast_fusion.1.refs_1_
  132.2 2.0 copy.217
  142.5 17.2 %shard_map.282 = (bf16[4,64,1024]{2,1,0:T(8,128)(2,1)S(1)}, bf16[2,128,512]{2,1,0:T(8,128)(2,1)S(1)}, bf16[2,128,512]{2,1,0:T(8,128)(2,1)S(1)}, bf16[2,128,1408]...) custom-call(bf16[4,64,1024]{2,1,0:T(8,128)(2,1)S(1)} %bitcast.656, bf16[2,128,512]{2,1,0:T(8,128)(2,1)S(1)} %copy-done.6, ...), custom_call_target="tpu_custom_call" | custom-call | tf_op jit(solution)/shard_map/pallas_call | solution.py:374
  165.4 2.4 copy.226
  171.4 2.1 copy.220
  176.5 8.4 %shard_map.283 = (bf16[4,128,256]{2,1,0:T(8,128)(2,1)S(1)}, bf16[2,128,256]{2,1,0:T(8,128)(2,1)S(1)}, bf16[2,128,512]{2,1,0:T(8,128)(2,1)S(1)}) custom-call(bf16[128,256]{1,0:T(8,128)(2,1)S(1)} %convolution_convert_fusion.1.refs_0_, bf16[128,256]{1,0:T(8,128)(2,1)S(1)} %copy-done.13, bf16[2,128,512]{2,1,0:T(8,128)(2,1)S(1)} %copy_bitcast_fusion.refs_2_), custom_call_target="tpu_custom_call" | custom-call | tf_op jit(solution)/shard_map/pallas_call | solution.py:374
  186.1 3.3 pad_maximum_fusion
  191.0 17.5 %while.41 = (s32[]{:T(128)}, f32[1,1,128,256]{2,3,1,0:T(8,128)S(1)}, f32[2,1,1,64,128]{4,3,2,1,0:T(8,128)S(1)}, bf16[2,1,1,64,128]{4,3,2,1,0:T(8,128)(2,1)}, bf1...) while((s32[]{:T(128)}, ...), condition=%wide.region_16.17_spmd.clone.clone, body=%wide.region_9.16_spmd.clone.sunk.clone | while | flops 141848576 | bytes 4776221 | solution.py:440
  196.1 2.3 fusion.303
  204.9 2.3 fusion.303
  209.1 2.3 fusion.90
  217.6 65.9 %shard_map.284 = (f32[2,128,2368]{2,1,0:T(8,128)S(1)}, bf16[4,32,1152]{2,1,0:T(8,128)(2,1)S(1)}, f32[8,24,128]{2,1,0:T(8,128)S(1)}, bf16[2,128,512]{2,1,0:T(8,128)(2,1)S(1)}, bf16[2,128,768]{2,1,0:T(8,128)(2,1)S(1)}) custom-call(bf16[4,128,2368]{2,1,0:T(8,128)(2,1)S(1)} %bitcast.652, bf16[4,32,1152]{2,1,0:T(8,128)(2,1)S(1)} %concatenate.47.refs_1_, ...), custom_call_target="tpu_custom_call" | custom-call | tf_op jit(solution)/shard_map/pallas_call | solution.py:374
  290.9 30.9 %shard_map.285 = (f32[2,128,768]{2,1,0:T(8,128)S(1)}, f32[8,24,256]{2,1,0:T(8,128)S(1)}, f32[4,24,128]{2,1,0:T(8,128)S(1)}) custom-call(bf16[4,128,768]{2,1,0:T(8,128)(2,1)S(1)} %bitcast.653, f32[4,24,256]{2,1,0:T(8,128)S(1)} %maximum_bitcast_fusion.refs_1_, f32[24,128]{1,0:T(8,128)S(1)} %reduce_sum.179.refs_2_), custom_call_target="tpu_custom_call" | custom-call | tf_op jit(solution)/shard_map/pallas_call | solution.py:374
  333.1 2.2 copy.281
  335.4 2.2 copy.282
  (329 shorter events, 99.7 us)
Async XLA Ops:
  0.6 35.6 %copy-start = (f32[16,512]{1,0:T(8,128)S(1)}, f32[16,512]{1,0:T(8,128)}, u32[]{:S(2)}) copy-start(f32[16,512]{1,0:T(8,128)} %param.28) | copy-start | bytes 98308
  5.2 29.3 %copy-start.22 = (f32[1,128,1024]{2,1,0:T(8,128)S(1)}, f32[1,128,1024]{2,1,0:T(8,128)}, u32[]{:S(2)}) copy-start(f32[1,128,1024]{2,1,0:T(8,128)} %param.20) | copy-start | bytes 1572868
  35.2 13.8 %copy-start.61 = (f32[128]{0:T(128)}, f32[128]{0:T(128)S(1)}, u32[]{:S(2)}) copy-start(f32[128]{0:T(128)S(1)} %get-tuple-element.616) | copy-start | bytes 1540
  35.4 15.4 %copy-start.59 = (f32[128,16]{0,1:T(8,128)}, f32[128,16]{0,1:T(8,128)S(1)}, u32[]{:S(2)}) copy-start(f32[128,16]{0,1:T(8,128)S(1)} %fusion.129) | copy-start | bytes 24580
  37.1 11.9 %copy-start.49 = (f32[1,1,128,128]{3,2,1,0:T(8,128)}, f32[1,1,128,128]{3,2,1,0:T(8,128)S(1)}, u32[]{:S(2)}) copy-start(f32[1,1,128,128]{3,2,1,0:T(8,128)S(1)} %reduce_window_sum.52) | copy-start | bytes 196612
  50.8 7.1 %copy-start.68 = (f32[256]{0:T(256)S(1)}, f32[256]{0:T(256)}, u32[]{:S(2)}) copy-start(f32[256]{0:T(256)} %param.30) | copy-start | bytes 3076
  57.7 8.6 %copy-start.25 = (f32[2,1,1,64,256]{4,3,2,1,0:T(8,128)}, f32[2,1,1,64,256]{4,3,2,1,0:T(8,128)S(1)}, u32[]{:S(2)}) copy-start(f32[2,1,1,64,256]{4,3,2,1,0:T(8,128)S(1)} %get-tuple-element.911) | copy-start | bytes 393220
  57.7 8.6 %copy-start.29 = (f32[2,1,1,64,128]{4,3,2,1,0:T(8,128)}, f32[2,1,1,64,128]{4,3,2,1,0:T(8,128)S(1)}, u32[]{:S(2)}) copy-start(f32[2,1,1,64,128]{4,3,2,1,0:T(8,128)S(1)} %get-tuple-element.912) | copy-start | bytes 196612
  57.7 8.6 %copy-start.31 = (f32[2,1,1,64,128]{4,3,2,1,0:T(8,128)}, f32[2,1,1,64,128]{4,3,2,1,0:T(8,128)S(1)}, u32[]{:S(2)}) copy-start(f32[2,1,1,64,128]{4,3,2,1,0:T(8,128)S(1)} %get-tuple-element.913) | copy-start | bytes 196612
  57.7 8.6 %copy-start.38 = (f32[2,1,1,64,128]{4,3,2,1,0:T(8,128)}, f32[2,1,1,64,128]{4,3,2,1,0:T(8,128)S(1)}, u32[]{:S(2)}) copy-start(f32[2,1,1,64,128]{4,3,2,1,0:T(8,128)S(1)} %get-tuple-element.914) | copy-start | bytes 196612
  57.7 8.6 %copy-start.44 = (f32[2,1,1,128,256]{4,3,2,1,0:T(8,128)}, f32[2,1,1,128,256]{4,3,2,1,0:T(8,128)S(1)}, u32[]{:S(2)}) copy-start(f32[2,1,1,128,256]{4,3,2,1,0:T(8,128)S(1)} %get-tuple-element.881) | copy-start | bytes 786436
  57.7 8.6 %copy-start.45 = (f32[2,1,1,64,256]{4,3,2,1,0:T(8,128)}, f32[2,1,1,64,256]{4,3,2,1,0:T(8,128)S(1)}, u32[]{:S(2)}) copy-start(f32[2,1,1,64,256]{4,3,2,1,0:T(8,128)S(1)} %get-tuple-element.352) | copy-start | bytes 393220
  142.5 19.0 %copy-start.23 = (f32[1,128,1024]{2,1,0:T(8,128)S(1)}, f32[1,128,1024]{2,1,0:T(8,128)}, u32[]{:S(2)}) copy-start(f32[1,128,1024]{2,1,0:T(8,128)} %param.20) | copy-start | bytes 1572868
  171.4 5.1 %copy-start.13 = (bf16[128,256]{1,0:T(8,128)(2,1)S(1)}, bf16[128,256]{1,0:T(8,128)(2,1)}, u32[]{:S(2)}) copy-start(bf16[128,256]{1,0:T(8,128)(2,1)} %copy-done.12) | copy-start | bytes 196612
  186.0 4.9 %copy-start.30 = (f32[2,1,1,64,128]{4,3,2,1,0:T(8,128)S(1)}, f32[2,1,1,64,128]{4,3,2,1,0:T(8,128)}, u32[]{:S(2)}) copy-start(f32[2,1,1,64,128]{4,3,2,1,0:T(8,128)} %copy-done.29) | copy-start | bytes 196612
  186.1 4.9 %copy-start.32 = (f32[2,1,1,64,128]{4,3,2,1,0:T(8,128)S(1)}, f32[2,1,1,64,128]{4,3,2,1,0:T(8,128)}, u32[]{:S(2)}) copy-start(f32[2,1,1,64,128]{4,3,2,1,0:T(8,128)} %copy-done.31) | copy-start | bytes 196612
  192.5 5.9 %copy-start.53 = (bf16[2,1,1,64,256]{4,3,2,1,0:T(8,128)(2,1)S(1)}, bf16[2,1,1,64,256]{4,3,2,1,0:T(8,128)(2,1)}, u32[]{:S(2)}) copy-start(bf16[2,1,1,64,256]{4,3,2,1,0:T(8,128)(2,1)} %get-tuple-element.891) | copy-start | bytes 196612 | tf_op jit(solution)/shard_map/transpose(jvp(vmap(vmap())))/while
  201.2 5.9 %copy-start.53 = (bf16[2,1,1,64,256]{4,3,2,1,0:T(8,128)(2,1)S(1)}, bf16[2,1,1,64,256]{4,3,2,1,0:T(8,128)(2,1)}, u32[]{:S(2)}) copy-start(bf16[2,1,1,64,256]{4,3,2,1,0:T(8,128)(2,1)} %get-tuple-element.891) | copy-start | bytes 196612 | tf_op jit(solution)/shard_map/transpose(jvp(vmap(vmap())))/while
  214.9 68.6 %copy-start.62 = (f32[128]{0:T(128)S(1)}, f32[128]{0:T(128)}, u32[]{:S(2)}) copy-start(f32[128]{0:T(128)} %copy-done.61) | copy-start | bytes 1540
  217.6 67.8 %copy-start.24 = (f32[1,128,1024]{2,1,0:T(8,128)S(1)}, f32[1,128,1024]{2,1,0:T(8,128)}, u32[]{:S(2)}) copy-start(f32[1,128,1024]{2,1,0:T(8,128)} %param.20) | copy-start | bytes 1572868
  217.6 67.8 %copy-start.43 = (f32[128,1024]{1,0:T(8,128)S(1)}, f32[128,1024]{1,0:T(8,128)}, u32[]{:S(2)}) copy-start(f32[128,1024]{1,0:T(8,128)} %bitcast_add_fusion.6) | copy-start | bytes 1572868
  217.6 67.8 %copy-start.72 = (f32[128]{0:T(128)S(1)}, f32[128]{0:T(128)}, u32[]{:S(2)}) copy-start(f32[128]{0:T(128)} %get-tuple-element.615) | copy-start | bytes 1540
  285.4 5.4 %copy-start.63 = (f32[1024]{0:T(1024)S(1)}, f32[1024]{0:T(1024)}, u32[]{:S(2)}) copy-start(f32[1024]{0:T(1024)} %get-tuple-element.533) | copy-start | bytes 12292
  287.6 43.2 %copy-start.3 = (f32[2,128,2368]{2,1,0:T(8,128)S(1)}, f32[2,128,2368]{2,1,0:T(8,128)}, u32[]{:S(2)}) copy-start(f32[2,128,2368]{2,1,0:T(8,128)} %copy-done.2) | copy-start | bytes 7274500
  (53 other events, 129.9 us)
where the time goes:
time: 340 us; the launch traced here: 339 us
  Pallas kernels  202 us (59%)
  local copies, waits for them, and re-layouts  68.9 us (20%)
  other arithmetic  40.9 us (12%)
  matrix products  24.3 us (7%)
    pallas_call x7, Pallas kernels, exchange(): pl.pallas_call(kernel, out_shape=out_shape, in_specs=[vmem] * len(items),...  202 us
    unnamed x152, local copies, waits for them, and re-layouts  34 us
    dot_general x6, other arithmetic, block_step(): jnp.einsum('id,jd,ijd->ij', query_blk, key_blk, spread, precision=highest)  8.45 us
    dot_general x5, matrix products, dot_t(): lax.dot_general(left, right, (((1,), (1,)), ((), ())), preferred_element_...  6.81 us

commit v1 on v0

--- a/solution.py
+++ b/solution.py
@@ -1,3 +1,5 @@
+from types import SimpleNamespace
+
 import jax
 import jax.numpy as jnp
 from jax import lax
@@ -8,6 +10,7 @@
 DK = 128
 DV = 256
 SPAN = 64
+SEQ, HEAD, DP = "seq", "head", "dp"
 
 
 epsilon = 1e-06
@@ -753,9 +756,933 @@
     )
 
 
+def fused_layer(axes, dims, args):
+    n, nh, nd = axes
+    tok, width, shard, kc, vc, hid, rank = dims
+    bf16, f32 = jnp.bfloat16, jnp.float32
+    half = shard // 2
+    nhalf = n * half
+    acols = 2 * kc + 2 * vc
+    cuts = ((0, kc), (kc, kc), (2 * kc, vc), (2 * kc + vc, vc))
+    qrows = tok // nh
+    hhid = hid // 2
+    hkv = vc // 2
+    scale = DK ** (-0.5)
+    levels = []
+    size = tok // 2
+    while size:
+        levels.append(size)
+        size //= 2
+    nl = len(levels) + 2
+    srows = rank * 2
+    trows = -(-(rank + 2) // 8) * 8
+    grow = vc // kc
+    mrows = -(-(rank + 1 + grow) // 8) * 8
+    dma = pltpu.SemaphoreType.DMA
+    n_gather = 6
+    n_sum = 5
+    n_ar = 4
+
+    out_shape = [
+        jax.ShapeDtypeStruct((tok, width), f32),
+        jax.ShapeDtypeStruct((tok, width), f32),
+        jax.ShapeDtypeStruct((shard, kc), f32),
+        jax.ShapeDtypeStruct((shard, kc), f32),
+        jax.ShapeDtypeStruct((shard, vc), f32),
+        jax.ShapeDtypeStruct((shard, vc), f32),
+        jax.ShapeDtypeStruct((vc, shard), f32),
+        jax.ShapeDtypeStruct((hid, shard), f32),
+        jax.ShapeDtypeStruct((hid, shard), f32),
+        jax.ShapeDtypeStruct((hid, shard), f32),
+        jax.ShapeDtypeStruct((rank, shard), f32),
+        jax.ShapeDtypeStruct((1, shard), f32),
+        jax.ShapeDtypeStruct((1, shard), f32),
+        jax.ShapeDtypeStruct((rank, nh * kc), f32),
+        jax.ShapeDtypeStruct((1, nh * kc), f32),
+        jax.ShapeDtypeStruct((1, vc), f32),
+    ]
+    anys = pl.BlockSpec(memory_space=pl.ANY)
+    vmem = pl.BlockSpec(memory_space=pltpu.VMEM)
+    out_specs = [anys] * 10 + [vmem] * 6
+    in_specs = [anys] * 7 + [vmem] * 3 + [anys] * 4
+
+    shapes = dict(
+        X=((tok, width), f32),
+        COT=((tok, width), f32),
+        WA=((width, acols), bf16),
+        SIDE=((srows, width), bf16),
+        WO=((vc, width), bf16),
+        WG=((hid, width), bf16),
+        WU=((hid, width), bf16),
+        WD=((hid, width), bf16),
+        XS=((nl, tok, DK), f32),
+        GS=((nl * tok, DK), f32),
+        QKVO=((tok, acols), f32),
+        PRE=((tok, kc), f32),
+        LOW=((tok, rank), f32),
+        AM=((tok, tok), f32),
+        ST=((vc, DK), bf16),
+        STL=((n, vc, DK), bf16),
+        DEC=((8, DK), f32),
+        DECL=((n, 8, DK), f32),
+        S0=((vc, DK), f32),
+        SG=((vc, DK), bf16),
+        SGL=((n, vc, DK), bf16),
+        LG=((vc, DK), f32),
+        O=((tok, vc), f32),
+        HRES=((tok, width), f32),
+        HN=((tok, width), bf16),
+        DRES=((tok, width), f32),
+        XN=((tok, width), bf16),
+        DMIX=((tok, vc), f32),
+        AST0=((nh, qrows, width), bf16),
+        ALD0=((nh, qrows, width), bf16),
+        ASM0=((nh, qrows, width), bf16),
+        AST1=((nh, qrows, width), bf16),
+        ALD1=((nh, qrows, width), bf16),
+        ASM1=((nh, qrows, width), bf16),
+        AST2=((nh, qrows, width), bf16),
+        ALD2=((nh, qrows, width), bf16),
+        ASM2=((nh, qrows, width), bf16),
+        AST3=((nh, qrows, width + 128), bf16),
+        ALD3=((nh, qrows, width + 128), bf16),
+        ASM3=((nh, qrows, width + 128), bf16),
+        HN2=((2 * tok, nhalf), bf16),
+        HNO=((tok, nhalf), bf16),
+        GO2=((2 * tok, nhalf), bf16),
+        GOO=((tok, nhalf), bf16),
+        DY2=((2 * tok, nhalf), bf16),
+        DYO=((tok, nhalf), bf16),
+        XN2=((2 * tok, nhalf), bf16),
+        XNO=((tok, nhalf), bf16),
+        DA1=((2 * tok, hid), bf16),
+        DA2=((2 * tok, hid), bf16),
+        MM=((2 * tok, hid), bf16),
+        ZZ=((2 * tok, vc), bf16),
+        DP=((2 * tok, acols), bf16),
+        RG=((hid, nhalf), bf16),
+        RU=((hid, nhalf), bf16),
+        RD=((hid, nhalf), bf16),
+        RO=((vc, nhalf), bf16),
+        RA=((nhalf, acols), bf16),
+        LG_=((2, 3, hid, half), bf16),
+        LU_=((2, 3, hid, half), bf16),
+        LD_=((2, 3, hid, half), bf16),
+        LO_=((2, 3, vc, half), bf16),
+        LA_=((2, 3, half, acols), bf16),
+        FG=((hid, half), f32),
+        FU=((hid, half), f32),
+        FD=((hid, half), f32),
+        FO=((vc, half), f32),
+        FA=((half, acols), f32),
+        BOUT=((tok, width), f32),
+        GIN=((tok, width), f32),
+        TALL=((n, trows, shard), f32),
+        TALLL=((n * nd, trows, shard), f32),
+        SMALL=((mrows, kc), f32),
+        SMALLL=((n * nd, mrows, kc), f32),
+        SMH=((mrows, kc), f32),
+        SMHL=((nh, mrows, kc), f32),
+    )
+    names = list(shapes)
+    scratch = [pltpu.VMEM(*shapes[name]) for name in names]
+    sem_shapes = dict(
+        load=(12,),
+        gat=(n_gather, 2, 2, n - 1),
+        gtwo=(n_gather, 2, 2, n - 1),
+        st=(2, n),
+        dec=(2, n),
+        sg=(2, n),
+        ara=(n_ar, 2, nh),
+        arb=(n_ar, 2, nh),
+        act=(2, 9),
+        rs=(n_sum, 2, 2, 3),
+        outl=(12,),
+        outr=(2, 8),
+        tall=(2, n * nd),
+        small=(2, n * nd),
+        smh=(2, nh),
+    )
+    sem_names = list(sem_shapes)
+    scratch += [dma(sem_shapes[name]) for name in sem_names]
+
+    def kernel(*refs):
+        (x_h, cot_h, side_h, wq_h, wk_h, wv_h, wog_h, wf_r, fb_r, gg_r, wo_h, wg_h, wu_h, wd_h) = refs[:14]
+        outs = refs[14:30]
+        (bout_h, gin_h, gq_h, gk_h, gv_h, gog_h, gwo_h, gg_h, gu_h, gd_h) = outs[:10]
+        (low_o, again_o, mgain_o, forget_o, bias_o, group_o) = outs[10:]
+        R = SimpleNamespace(**dict(zip(names, refs[30 : 30 + len(names)])))
+        S = SimpleNamespace(**dict(zip(sem_names, refs[30 + len(names) :])))
+        me, hh, dd = lax.axis_index(SEQ), lax.axis_index(HEAD), lax.axis_index(DP)
+        other = 1 - dd
+        mesh_id = pl.DeviceIdType.MESH
+
+        def remote(src, dst, send, recv, to):
+            return pltpu.make_async_remote_copy(
+                src_ref=src, dst_ref=dst, send_sem=send, recv_sem=recv, device_id=to, device_id_type=mesh_id
+            )
+
+        def mult(value, by):
+            return pl.multiple_of(value * by, by)
+
+        def lanes_of(place):
+            return pl.ds(mult(place, shard), shard)
+
+        late = []
+
+        rows_me = pl.ds(mult(me, shard), shard)
+        loads = [
+            (wq_h, R.WA.at[rows_me, 0:kc]),
+            (wk_h, R.WA.at[rows_me, kc : 2 * kc]),
+            (wv_h, R.WA.at[rows_me, 2 * kc : 2 * kc + vc]),
+            (wog_h, R.WA.at[rows_me, 2 * kc + vc : acols]),
+            (side_h, R.SIDE.at[:, lanes_of(me)]),
+            (x_h, R.X),
+            (wo_h, R.WO.at[:, lanes_of(me)]),
+            (wg_h, R.WG.at[:, lanes_of(me)]),
+            (wu_h, R.WU.at[:, lanes_of(me)]),
+            (wd_h, R.WD.at[:, lanes_of(me)]),
+            (cot_h, R.COT),
+        ]
+        loads = [pltpu.make_async_copy(a, b, S.load.at[i]) for i, (a, b) in enumerate(loads)]
+        for copy in loads:
+            copy.start()
+
+        barrier = pltpu.get_barrier_semaphore()
+        count = 0
+        for k in range(1, nh):
+            pl.semaphore_signal(barrier, inc=1, device_id={HEAD: lax.rem(hh + k, nh)}, device_id_type=mesh_id)
+            count += 1
+        flat = me * nd + dd
+        for k in range(1, n * nd):
+            peer = lax.rem(flat + k, n * nd)
+            pl.semaphore_signal(
+                barrier, inc=1, device_id={SEQ: peer // nd, DP: lax.rem(peer, nd)}, device_id_type=mesh_id
+            )
+            count += 1
+        pl.semaphore_wait(barrier, count)
+
+        def rows_view(ref, c, d):
+            return ref.at[pl.ds(pl.multiple_of(c * shard + d * half, half), half)]
+
+        def lane_view(rows):
+            return lambda ref, c, d: ref.at[pl.ds(mult(d, rows), rows), lanes_of(c)]
+
+        pieces = [
+            (R.WA, rows_view),
+            (R.SIDE, lane_view(rank)),
+            (R.WO, lane_view(hkv)),
+            (R.WG, lane_view(hhid)),
+            (R.WU, lane_view(hhid)),
+            (R.WD, lane_view(hhid)),
+        ]
+        open_ends = (me < n - 1, me > 0)
+
+        def guarded(ok, call):
+            late.append(lambda: pl.when(ok)(call))
+
+        def g_hop(p, way, step, c):
+            ref, view = pieces[p]
+            v = view(ref, c, dd)
+            return remote(v, v, S.gat.at[p, way, 0, step], S.gat.at[p, way, 1, step], {SEQ: me + 1 if way == 0 else me - 1})
+
+        def g_pair(p, way, step, c, d):
+            ref, view = pieces[p]
+            v = view(ref, c, d)
+            return remote(v, v, S.gtwo.at[p, way, 0, step], S.gtwo.at[p, way, 1, step], {DP: other})
+
+        def d_send(p, way, dist):
+            ref, view = pieces[p]
+            v = view(ref, me, dd)
+            to = me + dist if way == 0 else me - dist
+            return remote(v, v, S.gat.at[p, way, 0, dist - 1], S.gat.at[p, way, 1, dist - 1], {SEQ: to})
+
+        def reach(way, dist):
+            return me + dist < n if way == 0 else me - dist >= 0
+
+        def d_own(p):
+            for dist in range(min(2, n - 1), 0, -1):
+                for way in range(2):
+                    ok = reach(way, dist)
+                    pl.when(ok)(lambda way=way, dist=dist: d_send(p, way, dist).start())
+                    guarded(ok, lambda way=way, dist=dist: d_send(p, way, dist).wait_send())
+
+        def d_take(p, dist):
+            if dist >= n:
+                return
+            for way in range(2):
+                c, ok = came_of(way, dist - 1)
+                pl.when(ok)(lambda way=way, c=c: g_hop(p, way, dist - 1, c).wait_recv())
+                if dist == 2 and n > 3:
+                    on = jnp.logical_and(ok, open_ends[way])
+                    pl.when(on)(lambda way=way, c=c: g_hop(p, way, 2, c).start())
+                    guarded(on, lambda way=way, c=c: g_hop(p, way, 2, c).wait_send())
+                pl.when(ok)(lambda way=way, c=c: g_pair(p, way, dist - 1, c, dd).start())
+                guarded(ok, lambda way=way, c=c: g_pair(p, way, dist - 1, c, dd).wait_send())
+
+        def came_of(way, step):
+            c = me - 1 - step if way == 0 else me + 1 + step
+            return c, (c >= 0 if way == 0 else c < n)
+
+        def g_own(p):
+            for way in range(2):
+                pl.when(open_ends[way])(lambda way=way: g_hop(p, way, 0, me).start())
+                guarded(open_ends[way], lambda way=way: g_hop(p, way, 0, me).wait_send())
+
+        def g_step(p, step):
+            for way in range(2):
+                c, ok = came_of(way, step)
+                on = jnp.logical_and(ok, open_ends[way])
+                pl.when(ok)(lambda way=way, c=c: g_hop(p, way, step, c).wait_recv())
+                if step + 1 < n - 1:
+                    pl.when(on)(lambda way=way, c=c: g_hop(p, way, step + 1, c).start())
+                    guarded(on, lambda way=way, c=c: g_hop(p, way, step + 1, c).wait_send())
+                pl.when(ok)(lambda way=way, c=c: g_pair(p, way, step, c, dd).start())
+                guarded(ok, lambda way=way, c=c: g_pair(p, way, step, c, dd).wait_send())
+
+        def g_end(p):
+            for step in range(n - 1):
+                for way in range(2):
+                    c, ok = came_of(way, step)
+                    pl.when(ok)(lambda way=way, c=c, step=step: g_pair(p, way, step, c, other).wait_recv())
+
+        heads = (
+            (R.AST0, R.ALD0, R.ASM0),
+            (R.AST1, R.ALD1, R.ASM1),
+            (R.AST2, R.ALD2, R.ASM2),
+            (R.AST3, R.ALD3, R.ASM3),
+        )
+
+        def ar_refs(k):
+            return heads[k]
+
+        def ar_pair(k, sems, src, dst, j, to):
+            return remote(src, dst, sems.at[k, 0, j], sems.at[k, 1, j], {HEAD: to})
+
+        def ar_start(k):
+            src, land, _ = ar_refs(k)
+            for j in range(1, nh):
+                to = lax.rem(hh + j, nh)
+                copy = ar_pair(k, S.ara, src.at[to], land.at[hh], j, to)
+                copy.start()
+                late.append(copy.wait_send)
+
+        def ar_mid(k):
+            src, land, dst = ar_refs(k)
+            total = src[hh].astype(f32)
+            for j in range(1, nh):
+                came = lax.rem(hh + nh - j, nh)
+                ar_pair(k, S.ara, land.at[came], land.at[came], j, came).wait_recv()
+                total = total + land[came].astype(f32)
+            dst[hh] = total.astype(bf16)
+            for j in range(1, nh):
+                to = lax.rem(hh + j, nh)
+                copy = ar_pair(k, S.arb, dst.at[hh], dst.at[hh], j, to)
+                copy.start()
+                late.append(copy.wait_send)
+
+        def ar_end(k):
+            dst = ar_refs(k)[2]
+            for j in range(1, nh):
+                came = lax.rem(hh + nh - j, nh)
+                ar_pair(k, S.arb, dst.at[came], dst.at[came], j, came).wait_recv()
+
+        def ar_fill(k, value):
+            src = ar_refs(k)[0]
+            for j in range(nh):
+                src[j, :, : value.shape[1]] = value[j * qrows : (j + 1) * qrows].astype(bf16)
+
+        def ar_value(k, cols=width):
+            dst = ar_refs(k)[2]
+            return jnp.concatenate([dst[j, :, :cols] for j in range(nh)], axis=0).astype(f32)
+
+        def act_send(i, src, dst):
+            copy = remote(src, dst, S.act.at[0, i], S.act.at[1, i], {DP: other})
+            copy.start()
+            late.append(copy.wait_send)
+
+        def act_wait(i, src, dst):
+            remote(src, dst, S.act.at[0, i], S.act.at[1, i], {DP: other}).wait_recv()
+
+        top, low_rows = pl.ds(0, tok), pl.ds(tok, tok)
+
+        def split(value, mine, theirs):
+            for z in range(n):
+                lo = value[:, z * shard : z * shard + half]
+                hi = value[:, z * shard + half : (z + 1) * shard]
+                first = dd == 0
+                mine[0:tok, z * half : (z + 1) * half] = jnp.where(first, lo, hi)
+                theirs[:, z * half : (z + 1) * half] = jnp.where(first, hi, lo)
+
+        sums = [
+            (R.RG, R.LG_, R.FG, True),
+            (R.RU, R.LU_, R.FU, True),
+            (R.RD, R.LD_, R.FD, True),
+            (R.RO, R.LO_, R.FO, True),
+            (R.RA, R.LA_, R.FA, False),
+        ]
+
+        def chunk(p, g):
+            ref, kind = sums[p][0], sums[p][3]
+            at = g * half if isinstance(g, int) else mult(g, half)
+            if kind:
+                return ref.at[:, pl.ds(at, half)]
+            return ref.at[pl.ds(at, half)]
+
+        def r_send(p, way, slot, src, to):
+            return remote(
+                src, sums[p][1].at[way, slot], S.rs.at[p, way, 0, slot], S.rs.at[p, way, 1, slot], {SEQ: to}
+            )
+
+        ends = (me == 0, me == n - 1)
+        seconds = (me == 1, me == n - 2)
+
+        def r_start(p, way):
+            far = n - 1 if way == 0 else 0
+            step = 1 if way == 0 else -1
+            if n > 3:
+                pl.when(ends[way])(lambda: r_send(p, way, 2, chunk(p, far), me + step).start())
+                guarded(ends[way], lambda: r_send(p, way, 2, chunk(p, far), me + step).wait_send())
+            for dist in range(min(2, n - 1), 0, -1):
+                ok = reach(way, dist)
+                if dist == 2 and n > 3:
+                    ok = jnp.logical_and(ok, jnp.logical_not(seconds[way]))
+                to = me + dist * step
+                pl.when(ok)(lambda dist=dist, to=to: r_send(p, way, dist - 1, chunk(p, to), to).start())
+                guarded(ok, lambda dist=dist, to=to: r_send(p, way, dist - 1, chunk(p, to), to).wait_send())
+
+        def r_relay(p):
+            land = sums[p][1]
+            if n > 3:
+                for way in range(2):
+                    far = n - 1 if way == 0 else 0
+
+                    @pl.when(seconds[way])
+                    def _():
+                        r_send(p, way, 2, land.at[way, 2], me).wait_recv()
+                        land[way, 2] = (land[way, 2].astype(f32) + chunk(p, far)[...].astype(f32)).astype(bf16)
+                        r_send(p, way, 1, land.at[way, 2], far).start()
+
+                    guarded(seconds[way], lambda way=way, far=far: r_send(p, way, 1, land.at[way, 2], far).wait_send())
+
+        def r_close(p):
+            land, fin = sums[p][1], sums[p][2]
+            fin[...] = chunk(p, me)[...].astype(f32)
+            for dist in range(1, min(2, n - 1) + 1):
+                for way in range(2):
+
+                    @pl.when(reach(1 - way, dist))
+                    def _():
+                        r_send(p, way, dist - 1, land.at[way, dist - 1], me).wait_recv()
+                        fin[...] = fin[...] + land[way, dist - 1].astype(f32)
+
+        outputs = [
+            (R.FG, gg_h, True),
+            (R.FU, gu_h, True),
+            (R.FD, gd_h, True),
+            (R.FO, gwo_h, True),
+        ] + [(R.FA.at[:, at : at + w], ref, False) for (at, w), ref in zip(cuts, (gq_h, gk_h, gv_h, gog_h))]
+
+        def out_view(ref, kind, d):
+            place = pl.ds(mult(d, half), half)
+            return ref.at[:, place] if kind else ref.at[place]
+
+        def put(i):
+            src, ref, kind = outputs[i]
+            view = out_view(ref, kind, dd)
+            copy = pltpu.make_async_copy(src, view, S.outl.at[i])
+            copy.start()
+            late.append(copy.wait)
+            copy = remote(src, view, S.outr.at[0, i], S.outr.at[1, i], {DP: other})
+            copy.start()
+            late.append(copy.wait_send)
+            theirs = out_view(ref, kind, other)
+            late.append(remote(theirs, theirs, S.outr.at[0, i], S.outr.at[1, i], {DP: other}).wait_recv)
+
+        def put_local(i, src, ref):
+            copy = pltpu.make_async_copy(src, ref, S.outl.at[i])
+            copy.start()
+            late.append(copy.wait)
+
+        def hdot(a, b):
+            return jnp.dot(a, b, precision=highest, preferred_element_type=f32)
+
+        def hdot_t(a, b):
+            return lax.dot_general(a, b, (((1,), (1,)), ((), ())), precision=highest, preferred_element_type=f32)
+
+        def hdot_rows(a, b):
+            return lax.dot_general(a, b, (((0,), (0,)), ((), ())), precision=highest, preferred_element_type=f32)
+
+        def iota(axis):
+            return lax.broadcasted_iota(jnp.int32, (tok, tok), axis)
+
+        def span(level, i, t):
+            if level == nl - 2:
+                return t <= i
+            if level == nl - 1:
+                return t > i
+            b = levels[level]
+            r = (i & ~(2 * b - 1)) + (b - 1)
+            upper = (i & b) != 0
+            return jnp.logical_or(
+                jnp.logical_and(upper, jnp.logical_and(t > r, t <= i)),
+                jnp.logical_and(jnp.logical_not(upper), jnp.logical_and(t > i, t <= r)),
+            )
+
+        def mask_of(level):
+            b = levels[level]
+            i, j = iota(0), iota(1)
+            same = (i & ~(2 * b - 1)) == (j & ~(2 * b - 1))
+            return jnp.logical_and(same, jnp.logical_and((i & b) != 0, (j & b) == 0))
+
+        def upper_rows(level):
+            return (lax.broadcasted_iota(jnp.int32, (tok, DK), 0) & levels[level]) != 0
+
+        for copy in loads[:5]:
+            copy.wait()
+        g_own(1)
+        g_own(0)
+        loads[5].wait()
+        x = R.X[...]
+        scale_one = lax.rsqrt(jnp.mean(x * x, axis=-1, keepdims=True) + epsilon)
+        for step in range(n - 1):
+            g_step(1, step)
+            g_step(0, step)
+        for copy in loads[6:]:
+            copy.wait()
+        d_own(2)
+        d_own(3)
+        g_end(1)
+        gain_first = R.SIDE[rank : rank + 1].astype(f32)
+        normed = (x * scale_one * gain_first).astype(bf16)
+        R.XN[...] = normed
+        low = dot_t(normed, R.SIDE[0:rank])
+        R.LOW[...] = low
+        fcols = pl.ds(mult(hh, kc), kc)
+        pre = hdot(low, wf_r[:, fcols]) + fb_r[:, fcols]
+        R.PRE[...] = pre
+        decay = (jnp.minimum(pre, 0.0) - jnp.log1p(jnp.exp(-jnp.abs(pre)))) / normalizer
+        for level in range(nl):
+            ones = jnp.where(span(level, iota(0), iota(1)), 1.0, 0.0).astype(f32)
+            R.XS[level] = jnp.exp(hdot(ones, decay))
+        total_decay = jnp.exp(jnp.sum(decay, axis=0, keepdims=True))
+        R.DEC[...] = jnp.broadcast_to(total_decay, (8, DK))
+        g_end(0)
+        R.QKVO[...] = product(normed, R.WA[...])
+        keys = R.QKVO[:, kc : 2 * kc]
+        values = R.QKVO[:, 2 * kc : 2 * kc + vc]
+        R.ST[...] = hdot_rows(values, keys * R.XS[nl - 1]).astype(bf16)
+
+        def seq_pair(sems, src, dst, k, to):
+            return remote(src, dst, sems.at[0, k], sems.at[1, k], {SEQ: to})
+
+        for k in range(1, n):
+            to = lax.rem(me + k, n)
+            copy = seq_pair(S.dec, R.DEC, R.DECL.at[me], k, to)
+            copy.start()
+            late.append(copy.wait_send)
+            ok = me + k < n
+            pl.when(ok)(lambda k=k: seq_pair(S.st, R.ST, R.STL.at[me], k, me + k).start())
+            guarded(ok, lambda k=k: seq_pair(S.st, R.ST, R.STL.at[me], k, me + k).wait_send())
+        d_own(4)
+        d_own(5)
+
+        queries = R.QKVO[:, 0:kc] * scale
+        i, j = iota(0), iota(1)
+        scores = jnp.where(i == j, jnp.sum(queries * keys, axis=-1, keepdims=True), 0.0)
+        for level in range(nl - 2):
+            xs = R.XS[level]
+            up = upper_rows(level)
+            part = hdot_t(jnp.where(up, queries * xs, 0.0), jnp.where(up, 0.0, keys * xs))
+            scores = jnp.where(mask_of(level), part, scores)
+        R.AM[...] = scores
+        inside = hdot(scores, values)
+        split(R.XN[...], R.XN2, R.XNO)
+        split(R.COT[...].astype(bf16), R.GO2, R.GOO)
+        act_send(0, R.XNO, R.XN2.at[low_rows])
+        act_send(1, R.GOO, R.GO2.at[low_rows])
+        d_take(2, 1)
+        d_take(2, 2)
+        d_take(3, 2)
+
+        for k in range(1, n):
+            came = lax.rem(me + n - k, n)
+            seq_pair(S.dec, R.DECL.at[came], R.DECL.at[came], k, came).wait_recv()
+        R.S0[...] = jnp.zeros((vc, DK), f32)
+        for k in range(n - 1, 0, -1):
+
+            @pl.when(me - k >= 0)
+            def _():
+                src = me - k
+                seq_pair(S.st, R.STL.at[src], R.STL.at[src], k, src).wait_recv()
+                R.S0[...] = R.DECL[src, 0:1, :] * R.S0[...] + R.STL[src].astype(f32)
+
+        out = hdot_t(queries * R.XS[nl - 2], R.S0[...]) + inside
+        R.O[...] = out
+        gate = R.QKVO[:, 2 * kc + vc : acols]
+        sig3 = lax.logistic(gate)
+        scale_three = lax.rsqrt(jnp.mean(out * out, axis=-1, keepdims=True) + epsilon)
+        mixed = (out * scale_three * gg_r[...] * (gate * sig3)).astype(bf16)
+        R.ZZ[0:tok] = mixed
+        d_take(2, 3)
+        g_end(2)
+        ar_fill(0, product(mixed, R.WO[...]))
+        ar_start(0)
+        act_send(2, R.ZZ.at[top], R.ZZ.at[low_rows])
+        d_take(3, 1)
+        ar_mid(0)
+        d_take(4, 2)
+        ar_end(0)
+        hres = R.X[...] + ar_value(0)
+        R.HRES[...] = hres
+        scale_two = lax.rsqrt(jnp.mean(hres * hres, axis=-1, keepdims=True) + epsilon)
+        gain_second = R.SIDE[rank + 1 : rank + 2].astype(f32)
+        hn = (hres * scale_two * gain_second).astype(bf16)
+        R.HN[...] = hn
+        split(hn, R.HN2, R.HNO)
+        act_send(3, R.HNO, R.HN2.at[low_rows])
+        d_take(5, 2)
+        d_take(4, 1)
+        d_take(3, 3)
+        d_take(5, 1)
+        d_take(4, 3)
+        g_end(3)
+        g_end(4)
+        a1 = dot_t(R.HN[...], R.WG[...])
+        a2 = dot_t(R.HN[...], R.WU[...])
+        d_take(5, 3)
+        g_end(5)
+        d_hid = dot_t(R.COT[...].astype(bf16), R.WD[...])
+        s1 = lax.logistic(a1)
+        silu = a1 * s1
+        R.MM[0:tok] = (silu * a2).astype(bf16)
+        R.DA1[0:tok] = (d_hid * a2 * s1 * (1.0 + a1 * (1.0 - s1))).astype(bf16)
+        R.DA2[0:tok] = (d_hid * silu).astype(bf16)
+        ar_fill(1, product(R.DA1[0:tok], R.WG[...]) + product(R.DA2[0:tok], R.WU[...]))
+        ar_start(1)
+        act_send(4, R.DA1.at[top], R.DA1.at[low_rows])
+        act_send(5, R.DA2.at[top], R.DA2.at[low_rows])
+        act_send(6, R.MM.at[top], R.MM.at[low_rows])
+        ar_fill(2, product(R.MM[0:tok], R.WD[...]))
+        act_wait(1, R.GOO, R.GO2.at[low_rows])
+        act_wait(3, R.HNO, R.HN2.at[low_rows])
+        act_wait(4, R.DA1.at[top], R.DA1.at[low_rows])
+        R.RG[...] = dot_rows(R.DA1[...], R.HN2[...]).astype(bf16)
+        r_start(0, 0)
+        r_start(0, 1)
+        ar_mid(1)
+        ar_start(2)
+        act_wait(5, R.DA2.at[top], R.DA2.at[low_rows])
+        R.RU[...] = dot_rows(R.DA2[...], R.HN2[...]).astype(bf16)
+        r_start(1, 0)
+        act_wait(6, R.MM.at[top], R.MM.at[low_rows])
+        R.RD[...] = dot_rows(R.MM[...], R.GO2[...]).astype(bf16)
+        r_start(2, 0)
+        ar_end(1)
+
+        d_hn = ar_value(1)
+        hres = R.HRES[...]
+        scale_two = lax.rsqrt(jnp.mean(hres * hres, axis=-1, keepdims=True) + epsilon)
+        terms, d_norm = norm_back(hres, scale_two, gain_second, d_hn)
+        gain_two_grad = jnp.sum(terms, axis=0, keepdims=True)
+        d_res = R.COT[...] + d_norm
+        R.DRES[...] = d_res
+        dy = d_res.astype(bf16)
+        d_mixed = dot_t(dy, R.WO[...])
+        ar_mid(2)
+        out = R.O[...]
+        gate = R.QKVO[:, 2 * kc + vc : acols]
+        sig3 = lax.logistic(gate)
+        scale_three = lax.rsqrt(jnp.mean(out * out, axis=-1, keepdims=True) + epsilon)
+        normed_out = out * scale_three * gg_r[...]
+        d_on = d_mixed * (gate * sig3)
+        d_gate = d_mixed * normed_out * sig3 * (1.0 + gate * (1.0 - sig3))
+        R.DP[0:tok, 2 * kc + vc : acols] = d_gate.astype(bf16)
+        group_terms, d_out = norm_back(out, scale_three, gg_r[...], d_on)
+        group_row = jnp.sum(group_terms, axis=0, keepdims=True)
+        queries = R.QKVO[:, 0:kc] * scale
+        keys = R.QKVO[:, kc : 2 * kc]
+        values = R.QKVO[:, 2 * kc : 2 * kc + vc]
+        R.DMIX[...] = d_out
+        R.SG[...] = hdot_rows(d_out, queries * R.XS[nl - 2]).astype(bf16)
+        for k in range(1, n):
+            ok = me - k >= 0
+            pl.when(ok)(lambda k=k: seq_pair(S.sg, R.SG, R.SGL.at[me], k, me - k).start())
+            guarded(ok, lambda k=k: seq_pair(S.sg, R.SG, R.SGL.at[me], k, me - k).wait_send())
+        r_start(1, 1)
+        r_start(2, 1)
+        split(dy, R.DY2, R.DYO)
+        act_send(7, R.DYO, R.DY2.at[low_rows])
+
+        d_out = R.DMIX[...]
+        d_scores = hdot_t(d_out, values)
+        i, j = iota(0), iota(1)
+        diag = jnp.sum(jnp.where(i == j, d_scores, 0.0), axis=-1, keepdims=True)
+        d_q = diag * keys
+        d_k = diag * queries
+        for level in range(nl - 2):
+            xs = R.XS[level]
+            up = upper_rows(level)
+            part = jnp.where(mask_of(level), d_scores, 0.0)
+            q_part = xs * hdot(part, jnp.where(up, 0.0, keys * xs))
+            k_part = xs * hdot_rows(part, jnp.where(up, queries * xs, 0.0))
+            R.GS[level * tok : (level + 1) * tok] = queries * q_part + keys * k_part
+            d_q = d_q + q_part
+            d_k = d_k + k_part
+        q_part = R.XS[nl - 2] * hdot(d_out, R.S0[...])
+        R.GS[(nl - 2) * tok : (nl - 1) * tok] = queries * q_part
+        d_q = (d_q + q_part) * scale
+        R.DP[0:tok, 0:kc] = d_q.astype(bf16)
+        d_v = hdot_rows(R.AM[...], d_out)
+        r_relay(0)
+        R.LG[...] = jnp.zeros((vc, DK), f32)
+        for k in range(n - 1, 0, -1):
+
+            @pl.when(me + k < n)
+            def _():
+                src = me + k
+                seq_pair(S.sg, R.SGL.at[src], R.SGL.at[src], k, src).wait_recv()
+                R.LG[...] = R.DECL[src, 0:1, :] * R.LG[...] + R.SGL[src].astype(f32)
+
+        later = R.LG[...]
+        k_part = R.XS[nl - 1] * hdot(values, later)
+        R.GS[(nl - 1) * tok : nl * tok] = keys * k_part
+        R.DP[0:tok, kc : 2 * kc] = (d_k + k_part).astype(bf16)
+        d_v = d_v + hdot_t(keys * R.XS[nl - 1], later)
+        R.DP[0:tok, 2 * kc : 2 * kc + vc] = d_v.astype(bf16)
+        act_send(8, R.DP.at[top], R.DP.at[low_rows])
+        whole_row = R.DEC[0:1] * jnp.sum(R.S0[...] * later, axis=0, keepdims=True)
+        d_decay = jnp.broadcast_to(whole_row, (tok, DK))
+        for level in range(nl):
+            ones = jnp.where(span(level, iota(1), iota(0)), 1.0, 0.0).astype(f32)
+            d_decay = d_decay + hdot(ones, R.GS[level * tok : (level + 1) * tok])
+        d_pre = d_decay / normalizer * lax.logistic(-R.PRE[...])
+        src3 = R.AST3
+        src3[:, :, width:] = jnp.zeros((nh, qrows, 128), bf16)
+        d_low_part = hdot_t(d_pre, wf_r[:, fcols]).astype(bf16)
+        for k in range(nh):
+            src3[k, :, width : width + rank] = d_low_part[k * qrows : (k + 1) * qrows]
+        ar_fill(3, dot_t(R.DP[0:tok], R.WA[...]))
+        ar_start(3)
+        R.SMALL[...] = jnp.zeros((mrows, kc), f32)
+        R.SMALL[0:rank] = hdot_rows(R.LOW[...], d_pre)
+        R.SMALL[rank : rank + 1] = jnp.sum(d_pre, axis=0, keepdims=True)
+        for k in range(grow):
+            R.SMALL[rank + 1 + k : rank + 2 + k] = group_row[:, k * kc : (k + 1) * kc]
+
+        def all_pair(sems, src, dst, k, peer):
+            return remote(
+                src, dst, sems.at[0, k], sems.at[1, k], {SEQ: peer // nd, DP: lax.rem(peer, nd)}
+            )
+
+        for k in range(1, n * nd):
+            peer = lax.rem(flat + k, n * nd)
+            copy = all_pair(S.small, R.SMALL, R.SMALLL.at[flat], k, peer)
+            copy.start()
+            late.append(copy.wait_send)
+
+        r_relay(1)
+        act_wait(7, R.DYO, R.DY2.at[low_rows])
+        act_wait(2, R.ZZ.at[top], R.ZZ.at[low_rows])
+        R.RO[...] = dot_rows(R.ZZ[...], R.DY2[...]).astype(bf16)
+        act_wait(0, R.XNO, R.XN2.at[low_rows])
+        act_wait(8, R.DP.at[top], R.DP.at[low_rows])
+        R.RA[...] = dot_rows(R.XN2[...], R.DP[...]).astype(bf16)
+        for p in (3, 4):
+            r_start(p, 0)
+            r_start(p, 1)
+        ar_mid(3)
+        r_relay(2)
+        ar_end(2)
+        R.BOUT[...] = R.HRES[...] + ar_value(2)
+        put_local(8, R.BOUT, bout_h)
+        small = R.SMALL[...]
+        for k in range(1, n * nd):
+            came = lax.rem(flat + n * nd - k, n * nd)
+            all_pair(S.small, R.SMALLL.at[came], R.SMALLL.at[came], k, came).wait_recv()
+            small = small + R.SMALLL[came]
+        R.SMH[...] = small
+        R.SMHL[hh] = small
+        for k in range(1, nh):
+            to = lax.rem(hh + k, nh)
+            copy = remote(R.SMH, R.SMHL.at[hh], S.smh.at[0, k], S.smh.at[1, k], {HEAD: to})
+            copy.start()
+            late.append(copy.wait_send)
+        ar_end(3)
+        x = R.X[...]
+        scale_one = lax.rsqrt(jnp.mean(x * x, axis=-1, keepdims=True) + epsilon)
+        gain_first = R.SIDE[rank : rank + 1].astype(f32)
+        d_low = jnp.concatenate([R.ASM3[k, :, width : width + rank] for k in range(nh)], axis=0)
+        d_xn = ar_value(3) + product(d_low, R.SIDE[0:rank])
+        terms, d_norm = norm_back(x, scale_one, gain_first, d_xn)
+        gain_one_grad = jnp.sum(terms, axis=0, keepdims=True)
+        R.GIN[...] = R.DRES[...] + d_norm
+        put_local(9, R.GIN, gin_h)
+        low_grad = dot_rows(d_low, R.XN[...])
+        R.TALL[...] = jnp.zeros((n, trows, shard), f32)
+        for z in range(n):
+            cols = slice(z * shard, (z + 1) * shard)
+            R.TALL[z, 0:rank] = low_grad[:, cols]
+            R.TALL[z, rank : rank + 1] = gain_one_grad[:, cols]
+            R.TALL[z, rank + 1 : rank + 2] = gain_two_grad[:, cols]
+        for k in range(1, n * nd):
+            peer = lax.rem(flat + k, n * nd)
+            copy = all_pair(S.tall, R.TALL.at[peer // nd], R.TALLL.at[flat], k, peer)
+            copy.start()
+            late.append(copy.wait_send)
+        for p in range(3):
+            r_close(p)
+            put(p)
+        r_relay(3)
+        r_relay(4)
+        tall = R.TALL[me]
+        for k in range(1, n * nd):
+            came = lax.rem(flat + n * nd - k, n * nd)
+            all_pair(S.tall, R.TALLL.at[came], R.TALLL.at[came], k, came).wait_recv()
+            tall = tall + R.TALLL[came]
+        low_o[...] = tall[0:rank]
+        again_o[...] = tall[rank : rank + 1]
+        mgain_o[...] = tall[rank + 1 : rank + 2]
+        for k in range(1, nh):
+            came = lax.rem(hh + nh - k, nh)
+            remote(R.SMHL.at[came], R.SMHL.at[came], S.smh.at[0, k], S.smh.at[1, k], {HEAD: came}).wait_recv()
+        group = jnp.zeros((1, vc), f32)
+        for h in range(nh):
+            forget_o[:, h * kc : (h + 1) * kc] = R.SMHL[h, 0:rank]
+            bias_o[:, h * kc : (h + 1) * kc] = R.SMHL[h, rank : rank + 1]
+            group = group + jnp.concatenate(
+                [R.SMHL[h, rank + 1 + k : rank + 2 + k] for k in range(grow)], axis=1
+            )
+        group_o[...] = group
+        r_close(3)
+        put(3)
+        r_close(4)
+        for i in range(4, 8):
+            put(i)
+        for wait in late:
+            wait()
+
+    return pl.pallas_call(
+        kernel,
+        out_shape=out_shape,
+        in_specs=in_specs,
+        out_specs=out_specs,
+        scratch_shapes=scratch,
+        compiler_params=pltpu.CompilerParams(
+            collective_id=0, has_side_effects=True, vmem_limit_bytes=60 * 2**20
+        ),
+        name="fused_layer",
+    )(*args)
+
+
+def hand_over(arrays):
+    count = len(arrays)
+
+    def kernel(*refs):
+        ins, outs, held = refs[:count], refs[count : 2 * count], refs[2 * count : 3 * count]
+        sems = refs[3 * count]
+        taken = [pltpu.make_async_copy(a, b, sems.at[0, i]) for i, (a, b) in enumerate(zip(ins, held))]
+        given = [pltpu.make_async_copy(a, b, sems.at[1, i]) for i, (a, b) in enumerate(zip(held, outs))]
+        for copy in taken:
+            copy.start()
+        for first, second in zip(taken, given):
+            first.wait()
+            second.start()
+        for copy in given:
+            copy.wait()
+
+    anys = pl.BlockSpec(memory_space=pl.ANY)
+    return pl.pallas_call(
+        kernel,
+        out_shape=[jax.ShapeDtypeStruct(a.shape, a.dtype) for a in arrays],
+        in_specs=[anys] * count,
+        out_specs=[anys] * count,
+        scratch_shapes=[pltpu.VMEM(a.shape, a.dtype) for a in arrays] + [pltpu.SemaphoreType.DMA((2, count))],
+        compiler_params=pltpu.CompilerParams(vmem_limit_bytes=16 * 2**20),
+        name="hand_over",
+    )(*arrays)
+
+
+def one_kernel(
+    x_in, cotangent, attn_gain, w_query, w_key, w_value, w_outgate, w_lowrank, w_forget, forget_bias,
+    group_gain, w_output, mlp_gain, w_gate, w_up, w_down,
+):
+    n, nh, nd = lax.axis_size("seq"), lax.axis_size("head"), lax.axis_size("dp")
+    _, tok, width = x_in.shape
+    shard, rank = w_lowrank.shape
+    kc, vc, hid = w_query.shape[1], w_value.shape[1], w_gate.shape[1]
+    side = jnp.concatenate(
+        (w_lowrank.T, attn_gain[None, :], mlp_gain[None, :], jnp.zeros((rank - 2, shard), jnp.bfloat16)), axis=0
+    )
+    outs = fused_layer(
+        (n, nh, nd),
+        (tok, width, shard, kc, vc, hid, rank),
+        (
+            x_in.reshape(tok, width),
+            cotangent.reshape(tok, width),
+            side,
+            w_query,
+            w_key,
+            w_value,
+            w_outgate,
+            w_forget,
+            forget_bias[None, :],
+            group_gain[None, :],
+            w_output,
+            w_gate.T,
+            w_up.T,
+            w_down,
+        ),
+    )
+    (result, grad_in, gq, gk, gv, gog, gwo, gg, gu, gd, glow, gain1, gain2, gforget, gbias, ggroup) = hand_over(outs)
+    return (
+        result[None],
+        grad_in[None],
+        gain1[0],
+        gq,
+        gk,
+        gv,
+        gog,
+        glow.T,
+        gforget,
+        gbias[0],
+        ggroup[0],
+        gwo,
+        gain2[0],
+        gg.T,
+        gu.T,
+        gd,
+    )
+
+
+def fits_one_kernel(x_in, w_query, w_lowrank, w_value, w_gate):
+    seqs, tok, _ = x_in.shape
+    shard, rank = w_lowrank.shape
+    n_head, n_dp = lax.axis_size("head"), lax.axis_size("dp")
+    return (
+        seqs == 1
+        and n_dp == 2
+        and lax.axis_size("seq") in (2, 3, 4)
+        and tok & (tok - 1) == 0
+        and tok % (16 * n_head) == 0
+        and shard % 256 == 0
+        and w_query.shape[1] == DK
+        and w_value.shape[1] == DV
+        and w_gate.shape[1] % 32 == 0
+        and rank % 16 == 0
+    )
+
+
+def per_device(*args):
+    x_in, w_query, w_value, w_lowrank, w_gate = args[0], args[3], args[5], args[7], args[13]
+    if fits_one_kernel(x_in, w_query, w_lowrank, w_value, w_gate):
+        return one_kernel(*args)
+    return on_device(*args)
+
+
 def solution(mesh):
     return jax.shard_map(
-        on_device,
+        per_device,
         mesh=mesh,
         in_specs=(
             P("dp", "seq", None),

time: 340 us -> 162 us (0.48)
  local copies, waits for them, and re-layouts: 68.9 us -> 12.8 us
  Pallas kernels: 202 us -> 147 us
  other arithmetic: 40.9 us -> 0.68 us
  matrix products: 24.3 us -> 0 us
    pallas_call x7 -> x2, Pallas kernels: 202 us -> 147 us  [the longest x1 144 us: fused_layer(): pl.pallas_call(kernel, out_shape=out_shape, in_specs=in_specs, out_specs=...]
    dot_general x38 -> x0, matrix products: 24.3 us -> none  [the longest x5 6.81 us: dot_t(): lax.dot_general(left, right, (((1,), (1,)), ((), ())), preferred_element_...]
    unnamed x152 -> x38, local copies, waits for them, and re-layouts: 34 us -> 12.7 us
    dot_general x7 -> x0, other arithmetic: 9.26 us -> none  [the longest x6 8.45 us: block_step(): jnp.einsum('id,jd,ijd->ij', query_blk, key_blk, spread, precision=highest)]
    reduce_sum x14 -> x0, other arithmetic: 8.43 us -> none  [the longest x2 4.55 us: block_step(): running[:, None, :] - running[None, :, :]]
    reshape x5 -> x0, local copies, waits for them, and re-layouts: 6.58 us -> none  [the longest x1 2.07 us: on_device(): flat_cot = cotangent.reshape(total_rows, width)]
    split x4 -> x0, local copies, waits for them, and re-layouts: 5.01 us -> none  [the longest x2 3.54 us: on_device(): jnp.split(grads_attn, [key_cols, 2 * key_cols, 2 * key_cols + val_cols],...]
    concatenate x5 -> x1, local copies, waits for them, and re-layouts: 4.98 us -> 0.08 us  [one_kernel(): jnp.concatenate((w_lowrank.T, attn_gain[None, :], mlp_gain[None, :], jnp....]
where the time goes in v1:
time: 162 us
  Pallas kernels  147 us (91%)
  local copies, waits for them, and re-layouts  12.8 us (8%)
    pallas_call x1, Pallas kernels, fused_layer(): pl.pallas_call(kernel, out_shape=out_shape, in_specs=in_specs, out_specs=...  144 us
    unnamed x38, local copies, waits for them, and re-layouts  12.7 us
    pallas_call x1, Pallas kernels, hand_over(): pl.pallas_call(kernel, out_shape=[jax.ShapeDtypeStruct(a.shape, a.dtype)...  3.71 us

profile of v1, /device:TPU:0, one launch (start us, length us, event | category | flops | bytes accessed | tf_op | source)
XLA Modules:
  0.0 161.8 jit_solution(14638679406966253528)
XLA Ops:
  0.6 0.0 copy-start.16
  0.7 0.0 copy-start.17
  0.7 0.1 pad.3.clone
  0.8 0.6 copy-done.17
  1.3 0.6 copy-done.18
  2.0 0.0 copy-done.16
  2.0 0.7 maximum_maximum_fusion.refs_2_
  2.7 143.7 %fused_layer.1 = (f32[128,1024]{1,0:T(8,128)}, f32[128,1024]{1,0:T(8,128)}, f32[256,128]{1,0:T(8,128)}, f32[256,128]{1,0:T(8,128)}, f32[256,256]{1,0:T(8,128)}, ...) custom-call(f32[128,1024]{1,0:T(8,128)} %bitcast.16, ...), custom_call_target="tpu_custom_call" | custom-call | tf_op jit(solution)/shard_map/fused_layer/pallas_call | solution.py:1565
  146.3 0.0 copy-start.11
  146.4 0.7 copy-done.11
  147.0 0.0 copy-done.14
  147.1 0.0 copy-start
  147.1 1.1 copy-done
  148.2 1.1 copy-done.1
  149.3 1.1 copy-done.2
  150.4 1.0 copy-done.3
  151.4 1.0 copy-done.4
  152.5 0.9 copy-done.5
  153.4 0.9 copy-done.6
  154.4 0.9 copy-done.7
  155.3 0.9 copy-done.8
  156.2 0.9 copy-done.9
  157.1 0.8 copy-done.10
  157.9 3.7 %hand_over.1 = (f32[128,1024]{1,0:T(8,128)}, f32[128,1024]{1,0:T(8,128)}, f32[256,128]{1,0:T(8,128)}, f32[256,128]{1,0:T(8,128)}, f32[256,256]{1,0:T(8,128)}, /*...) custom-call(f32[128,1024]{1,0:T(8,128)S(1)} %copy-done.3, ...), custom_call_target="tpu_custom_call" | custom-call | tf_op jit(solution)/shard_map/hand_over/pallas_call | solution.py:1595
  (21 shorter events, 0.0 us)
Async XLA Ops:
  0.6 1.3 copy-start.16
  0.7 0.7 copy-start.17
  1.3 0.7 copy-start.18
  146.3 0.7 copy-start.11
  146.3 0.7 copy-start.14
  146.3 0.7 copy-start.15
  146.4 0.7 copy-start.12
  146.4 0.7 copy-start.13
  147.1 1.1 copy-start
  148.2 1.1 copy-start.1
  149.3 1.1 copy-start.2
  150.4 1.0 copy-start.3
  151.4 1.0 copy-start.4
  152.5 0.9 copy-start.5
  153.4 0.9 copy-start.6
  154.4 0.9 copy-start.7
  155.3 0.9 copy-start.8
  156.2 0.9 copy-start.9
  157.1 0.8 copy-start.10

commit v2 on v1

--- a/solution.py
+++ b/solution.py
@@ -1598,7 +1598,7 @@
         in_specs=[anys] * count,
         out_specs=[anys] * count,
         scratch_shapes=[pltpu.VMEM(a.shape, a.dtype) for a in arrays] + [pltpu.SemaphoreType.DMA((2, count))],
-        compiler_params=pltpu.CompilerParams(vmem_limit_bytes=16 * 2**20),
+        compiler_params=pltpu.CompilerParams(vmem_limit_bytes=60 * 2**20),
         name="hand_over",
     )(*arrays)
 

time: 162 us -> 151 us (0.932)
  local copies, waits for them, and re-layouts: 12.8 us -> 1.32 us
    unnamed x38 -> x6, local copies, waits for them, and re-layouts: 12.7 us -> 1.23 us
where the time goes in v2:
time: 151 us; the launch traced here: 150 us
  Pallas kernels  148 us (98%)
    pallas_call x1, Pallas kernels, fused_layer(): pl.pallas_call(kernel, out_shape=out_shape, in_specs=in_specs, out_specs=...  144 us
    pallas_call x1, Pallas kernels, hand_over(): pl.pallas_call(kernel, out_shape=[jax.ShapeDtypeStruct(a.shape, a.dtype)...  3.9 us

profile of v2, /device:TPU:0, one launch (start us, length us, event | category | flops | bytes accessed | tf_op | source)
XLA Modules:
  0.0 150.4 jit_solution(608794085692447147)
XLA Ops:
  0.6 0.0 copy-start
  0.7 0.0 copy-start.1
  0.7 0.1 pad.3.clone
  0.8 0.6 copy-done.1
  1.3 0.0 copy-start.2
  1.3 0.6 copy-done.2
  2.0 0.0 copy-done
  2.0 0.7 maximum_maximum_fusion.refs_2_
  2.7 143.7 %fused_layer.1 = (f32[128,1024]{1,0:T(8,128)}, f32[128,1024]{1,0:T(8,128)}, f32[256,128]{1,0:T(8,128)}, f32[256,128]{1,0:T(8,128)}, f32[256,256]{1,0:T(8,128)}, ...) custom-call(f32[128,1024]{1,0:T(8,128)} %bitcast.16, ...), custom_call_target="tpu_custom_call" | custom-call | tf_op jit(solution)/shard_map/fused_layer/pallas_call | solution.py:1565
  146.3 3.9 %hand_over.1 = (f32[128,1024]{1,0:T(8,128)}, f32[128,1024]{1,0:T(8,128)}, f32[256,128]{1,0:T(8,128)}, f32[256,128]{1,0:T(8,128)}, f32[256,256]{1,0:T(8,128)}, /*...) custom-call(f32[128,1024]{1,0:T(8,128)} %get-tuple-element.48.refs_0, ...), custom_call_target="tpu_custom_call" | custom-call | tf_op jit(solution)/shard_map/hand_over/pallas_call | solution.py:1595
  (3 shorter events, 0.0 us)
Async XLA Ops:
  0.6 1.3 copy-start
  0.7 0.7 copy-start.1
  1.3 0.7 copy-start.2
